TPU v7x, 256 devices: a whole 4x4x8 slice. The times are simulated.
256 devices in a mesh: ta: 8 (over z), ha: 4 (over x_hi, core), wa: 8 (over x_lo, y).
Axes of the slice: x: 4 (x_hi: 2, x_lo: 2; x = x_hi * 2 + x_lo), y: 4, z: 8, core: 2. Of those that a mesh axis runs over, the one named last changes fastest.
Arguments:
- features: bfloat16 [32, 64, 128, 256], P('ta', 'ha', 'wa'), may hold values from -6 to 6
- norm_gain: float32 [256], replicated, may hold values from 0.5 to 1.5
- conv_weight: bfloat16 [3, 3, 3, 256, 256], replicated, may hold values from -0.078125 to 0.078125
- cotangent: bfloat16 [32, 64, 128, 256], P('ta', 'ha', 'wa'), may hold values from -6 to 6
Outputs:
- decoded: bfloat16 [32, 64, 128, 256], P('ta', 'ha', 'wa')
- grad_features: bfloat16 [32, 64, 128, 256], P('ta', 'ha', 'wa')
- grad_weight: float32 [3, 3, 3, 256, 256], P(None, None, None, None, ('ha', 'wa'))
All inputs are finite; a program needn't handle non-finite values.
Results may differ from a plain program's by a relative error of at most 0.0032.
Values may be sent and summed in bfloat16 or wider, within the bound.
A program may use at most 128 MiB of HBM per device.

v0:
```python
import jax
import jax.numpy as jnp
from jax import lax
from jax.sharding import PartitionSpec as P

EPSILON = 1e-06


def from_behind(array, axis, by):
    length = lax.axis_size(axis)
    pairs = [(i, i + by) for i in range(length) if 0 <= i + by < length]
    return lax.ppermute(array, axis, pairs)


def with_halo(cells, sides, width):
    for axis, dim in sides:
        count = lax.axis_size(axis)
        ends = count - 1
        head = lax.slice_in_dim(cells, 0, width, axis=dim)
        tail = lax.slice_in_dim(cells, cells.shape[dim] - width, cells.shape[dim], axis=dim)
        cells = jnp.concatenate(
            [
                lax.ppermute(tail, axis, [(i, (i + 1) % count) for i in range(ends)]),
                cells,
                lax.ppermute(head, axis, [((i + 1) % count, i) for i in range(ends)]),
            ],
            axis=dim,
        )
    return cells


def activate(features, norm_gain):
    values = features.astype(jnp.float32)
    inverse = lax.rsqrt(jnp.mean(values * values, axis=-1, keepdims=True) + EPSILON)
    unit_rms = values * inverse
    normed = unit_rms * norm_gain
    activated = (normed * jax.nn.sigmoid(normed)).astype(jnp.bfloat16)
    return (values, inverse, unit_rms, normed, activated)


def norm_backward(grad_act, normed, unit_rms, inverse, norm_gain):
    logistic = jax.nn.sigmoid(normed)
    grad_normed = grad_act * logistic * (1.0 + normed * (1.0 - logistic))
    grad_unit = grad_normed * norm_gain
    return inverse * (grad_unit - unit_rms * jnp.mean(grad_unit * unit_rms, axis=-1, keepdims=True))


def body(features, norm_gain, conv_weight, cotangent):
    frames, height, width, channels = features.shape
    values, inverse, unit_rms, normed, activated = activate(features, norm_gain)
    earlier = from_behind(activated[frames - 2 :], "ta", 1)
    padded = with_halo(jnp.concatenate([earlier, activated], 0), (("ha", 1), ("wa", 2)), 1)
    later = from_behind(cotangent[:2], "ta", -1)
    grad_padded = with_halo(jnp.concatenate([cotangent, later], 0), (("ha", 1), ("wa", 2)), 1)
    flat_grad = cotangent.reshape(-1, channels)
    mixed = jnp.zeros((frames * height * width, channels), jnp.float32)
    grad_act = jnp.zeros((frames * height * width, channels), jnp.float32)
    windows = []
    for t_off in range(3):
        for h_off in range(3):
            for w_off in range(3):
                window = padded[
                    t_off : t_off + frames, h_off : h_off + height, w_off : w_off + width
                ].reshape(-1, channels)
                windows.append(window)
                mixed = mixed + jnp.dot(
                    window, conv_weight[t_off, h_off, w_off], preferred_element_type=jnp.float32
                )
                back = grad_padded[
                    2 - t_off : 2 - t_off + frames,
                    2 - h_off : 2 - h_off + height,
                    2 - w_off : 2 - w_off + width,
                ].reshape(-1, channels)
                grad_act = grad_act + lax.dot_general(
                    back,
                    conv_weight[t_off, h_off, w_off],
                    (((1,), (1,)), ((), ())),
                    preferred_element_type=jnp.float32,
                )
    owners = lax.axis_size("ha") * lax.axis_size("wa")
    owned = channels // owners
    weight_taps = jnp.stack(
        [
            lax.dot_general(
                window, flat_grad, (((0,), (0,)), ((), ())), preferred_element_type=jnp.float32
            )
            for window in windows
        ]
    )
    shared = lax.psum_scatter(weight_taps, ("ha", "wa"), scatter_dimension=2, tiled=True)
    summed = lax.psum(shared, "ta")
    voxels_all = (
        frames * height * width * lax.axis_size("ta") * lax.axis_size("ha") * lax.axis_size("wa")
    )
    grad_weight = summed.reshape(3, 3, 3, channels, owned) * float(voxels_all) ** (-0.5)
    decoded = (values + mixed.reshape(features.shape)).astype(jnp.bfloat16)
    grad_norm = norm_backward(
        grad_act.reshape(features.shape), normed, unit_rms, inverse, norm_gain
    )
    grad_features = (cotangent.astype(jnp.float32) + grad_norm).astype(jnp.bfloat16)
    return (decoded, grad_features, grad_weight)


def solution(mesh):
    placed = (P("ta", "ha", "wa", None), P(), P(), P("ta", "ha", "wa", None))
    return jax.shard_map(
        body,
        mesh=mesh,
        in_specs=placed,
        out_specs=(
            P("ta", "ha", "wa", None),
            P("ta", "ha", "wa", None),
            P(None, None, None, None, ("ha", "wa")),
        ),
        check_vma=False,
    )
```

profile of v0, /device:TPU:2, one launch (start us, length us, event | category | flops | bytes accessed | tf_op | source)
XLA Modules:
  0.0 364.5 jit_solution(647792730584632596)
XLA Ops:
  7.2 1.0 slice.400
  8.2 1.3 collective-permute-start.5
  9.5 1.1 constant_dynamic-update-slice_fusion.1
  10.6 1.3 fusion.49
  11.8 6.5 %collective-permute-done.5 = bf16[2,16,16,256]{3,2,1,0:T(8,128)(2,1)S(1)} collective-permute-done((bf16[2,16,16,256]{3,2,1,0:T(8,128)(2,1)S(1)}, bf16[2,16,16,256]{3,2,1,0:T(8,128)(2,1)S(1)}, u32[]{:S(2)}, u32[]{:S(2)}) %collective-permute-start.5) | collective-permute-done | bytes 262176 | tf_op jit(solution)/shard_map/ppermute | solution.py:12
  18.3 1.3 collective-permute-start.6
  19.6 1.3 collective-permute-start.7
  21.0 4.1 %collective-permute-done.7 = bf16[6,1,16,256]{3,2,1,0:T(8,128)(2,1)S(1)} collective-permute-done((bf16[6,1,16,256]{3,2,1,0:T(8,128)(2,1)S(1)}, bf16[6,1,16,256]{3,2,1,0:T(8,128)(2,1)S(1)}, u32[]{:S(2)}, u32[]{:S(2)}) %collective-permute-start.7) | collective-permute-done | bytes 49184 | tf_op jit(solution)/shard_map/ppermute | solution.py:25
  25.3 5.8 %collective-permute-start.8 = (bf16[6,18,1,256]{3,2,1,0:T(2,128)(2,1)S(1)}, bf16[6,18,1,256]{3,2,1,0:T(2,128)(2,1)S(1)}, u32[]{:S(2)}, u32[]{:S(2)}) collective-permute-start(bf16[6,18,1,256]{3,2,1,0:T(2,128)(2,1)S(1)} %get-tuple-element.47), channel_id=1, source_target_pairs={{1,0},{2,1},{3,2},{4,3},{5,4},{6,5},{7,6},{9,8},{10,9},{11,10},{12... | collective-permute-start | bytes 165896 | tf_op jit(solution)/shard_map/ppermute | solution.py:25
  31.1 1.9 collective-permute-start.9
  33.0 0.6 pad_maximum_fusion.4
  34.0 5.9 %collective-permute-done.9 = bf16[6,18,1,256]{3,2,1,0:T(2,128)(2,1)S(1)} collective-permute-done((bf16[6,18,1,256]{3,2,1,0:T(2,128)(2,1)S(1)}, bf16[6,18,1,256]{3,2,1,0:T(2,128)(2,1)S(1)}, u32[]{:S(2)}, u32[]{:S(2)}) %collective-permute-start.9) | collective-permute-done | bytes 55328 | tf_op jit(solution)/shard_map/ppermute | solution.py:23
  39.9 0.9 pad_maximum_fusion.1
  40.7 3.3 fusion.191
  51.5 0.4 copy-done.4
  53.2 0.3 copy-done.2
  53.5 0.7 fusion.44
  54.3 1.6 fusion.48
  55.9 3.8 %collective-permute-start = (bf16[2,16,16,256]{3,2,1,0:T(8,128)(2,1)S(1)}, bf16[2,16,16,256]{3,2,1,0:T(8,128)(2,1)S(1)}, u32[]{:S(2)}, u32[]{:S(2)}) collective-permute-start(bf16[2,16,16,256]{3,2,1,0:T(8,128)(2,1)S(1)} %slice.431), channel_id=1, source_target_pairs={{0,32},{32,64},{64,96},{96,128},{128,160},{160,192},{192,224},{1,3... | collective-permute-start | bytes 786440 | tf_op jit(solution)/shard_map/ppermute | solution.py:12
  59.7 4.7 %collective-permute-done = bf16[2,16,16,256]{3,2,1,0:T(8,128)(2,1)S(1)} collective-permute-done((bf16[2,16,16,256]{3,2,1,0:T(8,128)(2,1)S(1)}, bf16[2,16,16,256]{3,2,1,0:T(8,128)(2,1)S(1)}, u32[]{:S(2)}, u32[]{:S(2)}) %collective-permute-start) | collective-permute-done | bytes 262176 | tf_op jit(solution)/shard_map/ppermute | solution.py:12
  64.4 1.3 collective-permute-start.2
  65.7 4.6 %collective-permute-start.1 = (bf16[6,1,16,256]{3,2,1,0:T(8,128)(2,1)S(1)}, bf16[6,1,16,256]{3,2,1,0:T(8,128)(2,1)S(1)}, u32[]{:S(2)}, u32[]{:S(2)}) collective-permute-start(bf16[6,1,16,256]{3,2,1,0:T(8,128)(2,1)S(1)} %get-tuple-element.77), channel_id=1, source_target_pairs={{0,8},{8,16},{16,24},{1,9},{9,17},{17,25},{2,10},{10,18},{18,26},{... | collective-permute-start | bytes 147464 | tf_op jit(solution)/shard_map/ppermute | solution.py:23
  70.3 0.9 collective-permute-done.1
  71.4 1.9 collective-permute-start.4
  73.3 4.1 %collective-permute-start.3 = (bf16[6,18,1,256]{3,2,1,0:T(2,128)(2,1)S(1)}, bf16[6,18,1,256]{3,2,1,0:T(2,128)(2,1)S(1)}, u32[]{:S(2)}, u32[]{:S(2)}) collective-permute-start(bf16[6,18,1,256]{3,2,1,0:T(2,128)(2,1)S(1)} %get-tuple-element.52), channel_id=1, source_target_pairs={{0,1},{1,2},{2,3},{3,4},{4,5},{5,6},{6,7},{8,9},{9,10},{10,11},{11... | collective-permute-start | bytes 165896 | tf_op jit(solution)/shard_map/ppermute | solution.py:23
  77.4 0.6 collective-permute-done.4
  78.0 4.0 %collective-permute-done.3 = bf16[6,18,1,256]{3,2,1,0:T(2,128)(2,1)S(1)} collective-permute-done((bf16[6,18,1,256]{3,2,1,0:T(2,128)(2,1)S(1)}, bf16[6,18,1,256]{3,2,1,0:T(2,128)(2,1)S(1)}, u32[]{:S(2)}, u32[]{:S(2)}) %collective-permute-start.3) | collective-permute-done | bytes 55328 | tf_op jit(solution)/shard_map/ppermute | solution.py:23
  82.0 0.9 pad_maximum_fusion
  83.0 1.1 fusion.30
  84.1 1.1 fusion.36
  85.1 1.0 fusion.29
  86.2 1.0 fusion.28
  87.2 1.0 fusion.11
  88.3 1.0 fusion.27
  89.3 1.1 fusion.26
  90.3 1.1 fusion.35
  91.4 1.1 fusion.25
  92.5 1.0 fusion.24
  93.5 1.0 fusion.34
  94.5 1.0 fusion.23
  95.6 1.0 fusion.22
  96.6 1.0 fusion.10
  97.6 1.1 fusion.21
  98.7 1.0 fusion.20
  99.7 1.1 fusion.33
  100.8 1.1 fusion.19
  101.9 1.0 fusion.18
  102.9 1.1 fusion.32
  104.0 1.1 fusion.17
  105.0 1.0 fusion.16
  106.1 1.0 fusion.15
  107.1 1.1 fusion.14
  108.1 1.0 fusion.13
  109.2 1.1 fusion.31
  110.2 1.0 fusion.12
  111.3 10.3 %copy.10 = f32[27,256,256]{1,0,2:T(8,128)} copy(f32[27,256,256]{2,1,0:T(8,128)} %fusion.12) | data formatting | bytes 14155776 | tf_op jit(solution)/shard_map/stack | solution.py:82
  122.3 1.6 copy-done.1
  124.3 0.4 fusion.194
  125.1 0.9 fusion.193
  133.5 146.3 %reduce-scatter.2.cloned.1.call-done = f32[27,256,8]{1,0,2:T(8,128)} async-done(((f32[27,256,256]{1,0,2:T(8,128)}), f32[27,256,8]{1,0,2:T(8,128)}) %reduce-scatter.2.cloned.1.call-update) | async-done | bytes 221200 | tf_op jit(solution)/shard_map/reduce_scatter | solution.py:90
  279.8 1.8 copy.11
  281.6 1.0 fusion.50
  282.6 73.5 %all-reduce.2.cloned.1.call-done = f32[27,256,8]{1,2,0:T(8,128)} async-done(((f32[27,256,8]{1,2,0:T(8,128)}), f32[27,256,8]{1,2,0:T(8,128)}) %all-reduce.2.cloned.1.call-update) | async-done | bytes 221200 | tf_op jit(solution)/shard_map/psum | solution.py:91
  356.0 1.6 broadcast_multiply_fusion
  (82 shorter events, 18.2 us)
Async XLA Ops:
  7.2 272.6 %reduce-scatter.2.cloned.1.call-start = ((), (), s32[]{:S(2)}) async-start(), calls=%async_computation.1 | async-start | bytes 8650752 | tf_op jit(solution)/shard_map/reduce_scatter | solution.py:90
  8.2 10.1 %collective-permute-start.5 = (bf16[2,16,16,256]{3,2,1,0:T(8,128)(2,1)S(1)}, bf16[2,16,16,256]{3,2,1,0:T(8,128)(2,1)S(1)}, u32[]{:S(2)}, u32[]{:S(2)}) collective-permute-start(bf16[2,16,16,256]{3,2,1,0:T(8,128)(2,1)S(1)} %slice.400), channel_id=1, source_target_pairs={{32,0},{64,32},{96,64},{128,96},{160,128},{192,160},{224,192},{33,... | collective-permute-start | bytes 786440 | tf_op jit(solution)/shard_map/ppermute | solution.py:12
  18.3 2.6 collective-permute-start.6
  19.6 5.5 %collective-permute-start.7 = (bf16[6,1,16,256]{3,2,1,0:T(8,128)(2,1)S(1)}, bf16[6,1,16,256]{3,2,1,0:T(8,128)(2,1)S(1)}, u32[]{:S(2)}, u32[]{:S(2)}) collective-permute-start(bf16[6,1,16,256]{3,2,1,0:T(8,128)(2,1)S(1)} %get-tuple-element.71), channel_id=1, source_target_pairs={{8,0},{16,8},{24,16},{9,1},{17,9},{25,17},{10,2},{18,10},{26,18},{... | collective-permute-start | bytes 147464 | tf_op jit(solution)/shard_map/ppermute | solution.py:25
  21.0 12.7 %copy-start = (bf16[3,3,3,256,256]{4,3,2,1,0:T(8,128)(2,1)S(1)}, bf16[3,3,3,256,256]{4,3,2,1,0:T(8,128)(2,1)}, u32[]{:S(2)}) copy-start(bf16[3,3,3,256,256]{4,3,2,1,0:T(8,128)(2,1)} %param.6) | copy-start | bytes 10616836
  25.3 8.7 %collective-permute-start.8 = (bf16[6,18,1,256]{3,2,1,0:T(2,128)(2,1)S(1)}, bf16[6,18,1,256]{3,2,1,0:T(2,128)(2,1)S(1)}, u32[]{:S(2)}, u32[]{:S(2)}) collective-permute-start(bf16[6,18,1,256]{3,2,1,0:T(2,128)(2,1)S(1)} %get-tuple-element.47), channel_id=1, source_target_pairs={{1,0},{2,1},{3,2},{4,3},{5,4},{6,5},{7,6},{9,8},{10,9},{11,10},{12... | collective-permute-start | bytes 165896 | tf_op jit(solution)/shard_map/ppermute | solution.py:25
  31.1 8.8 %collective-permute-start.9 = (bf16[6,18,1,256]{3,2,1,0:T(2,128)(2,1)S(1)}, bf16[6,18,1,256]{3,2,1,0:T(2,128)(2,1)S(1)}, u32[]{:S(2)}, u32[]{:S(2)}) collective-permute-start(bf16[6,18,1,256]{3,2,1,0:T(2,128)(2,1)S(1)} %get-tuple-element.48), channel_id=1, source_target_pairs={{0,1},{1,2},{2,3},{3,4},{4,5},{5,6},{6,7},{8,9},{9,10},{10,11},{11... | collective-permute-start | bytes 165896 | tf_op jit(solution)/shard_map/ppermute | solution.py:23
  50.8 1.0 copy-start.4
  52.5 1.0 copy-start.2
  52.5 1.0 copy-start.5
  55.9 8.5 %collective-permute-start = (bf16[2,16,16,256]{3,2,1,0:T(8,128)(2,1)S(1)}, bf16[2,16,16,256]{3,2,1,0:T(8,128)(2,1)S(1)}, u32[]{:S(2)}, u32[]{:S(2)}) collective-permute-start(bf16[2,16,16,256]{3,2,1,0:T(8,128)(2,1)S(1)} %slice.431), channel_id=1, source_target_pairs={{0,32},{32,64},{64,96},{96,128},{128,160},{160,192},{192,224},{1,3... | collective-permute-start | bytes 786440 | tf_op jit(solution)/shard_map/ppermute | solution.py:12
  64.4 5.9 %collective-permute-start.2 = (bf16[6,1,16,256]{3,2,1,0:T(8,128)(2,1)S(1)}, bf16[6,1,16,256]{3,2,1,0:T(8,128)(2,1)S(1)}, u32[]{:S(2)}, u32[]{:S(2)}) collective-permute-start(bf16[6,1,16,256]{3,2,1,0:T(8,128)(2,1)S(1)} %get-tuple-element.76), channel_id=1, source_target_pairs={{8,0},{16,8},{24,16},{9,1},{17,9},{25,17},{10,2},{18,10},{26,18},{... | collective-permute-start | bytes 147464 | tf_op jit(solution)/shard_map/ppermute | solution.py:25
  65.7 5.4 %collective-permute-start.1 = (bf16[6,1,16,256]{3,2,1,0:T(8,128)(2,1)S(1)}, bf16[6,1,16,256]{3,2,1,0:T(8,128)(2,1)S(1)}, u32[]{:S(2)}, u32[]{:S(2)}) collective-permute-start(bf16[6,1,16,256]{3,2,1,0:T(8,128)(2,1)S(1)} %get-tuple-element.77), channel_id=1, source_target_pairs={{0,8},{8,16},{16,24},{1,9},{9,17},{17,25},{2,10},{10,18},{18,26},{... | collective-permute-start | bytes 147464 | tf_op jit(solution)/shard_map/ppermute | solution.py:23
  71.4 6.6 %collective-permute-start.4 = (bf16[6,18,1,256]{3,2,1,0:T(2,128)(2,1)S(1)}, bf16[6,18,1,256]{3,2,1,0:T(2,128)(2,1)S(1)}, u32[]{:S(2)}, u32[]{:S(2)}) collective-permute-start(bf16[6,18,1,256]{3,2,1,0:T(2,128)(2,1)S(1)} %get-tuple-element.51), channel_id=1, source_target_pairs={{1,0},{2,1},{3,2},{4,3},{5,4},{6,5},{7,6},{9,8},{10,9},{11,10},{12... | collective-permute-start | bytes 165896 | tf_op jit(solution)/shard_map/ppermute | solution.py:25
  73.3 8.8 %collective-permute-start.3 = (bf16[6,18,1,256]{3,2,1,0:T(2,128)(2,1)S(1)}, bf16[6,18,1,256]{3,2,1,0:T(2,128)(2,1)S(1)}, u32[]{:S(2)}, u32[]{:S(2)}) collective-permute-start(bf16[6,18,1,256]{3,2,1,0:T(2,128)(2,1)S(1)} %get-tuple-element.52), channel_id=1, source_target_pairs={{0,1},{1,2},{2,3},{3,4},{4,5},{5,6},{6,7},{8,9},{9,10},{10,11},{11... | collective-permute-start | bytes 165896 | tf_op jit(solution)/shard_map/ppermute | solution.py:23
  121.6 234.4 %all-reduce.2.cloned.1.call-start = ((), (), s32[]{:S(2)}) async-start(), calls=%async_computation.2 | async-start | bytes 442368 | tf_op jit(solution)/shard_map/psum | solution.py:91
  121.9 2.0 copy-start.1
  132.9 148.7 %copy-start.3 = (bf16[4,16,16,256]{3,2,1,0:T(8,128)(2,1)S(1)}, bf16[4,16,16,256]{3,2,1,0:T(8,128)(2,1)}, u32[]{:S(2)}) copy-start(bf16[4,16,16,256]{3,2,1,0:T(8,128)(2,1)} %param.4) | copy-start | bytes 1572868
Sparse Core Ops, SparseCore 0:
  121.7 158.0 reduce-scatter.1
  282.7 73.2 all-reduce.1
where the time goes:
time: 365 us; the launch traced here: 364 us
  waiting for transfers between devices  246 us (67%)
  matrix products  45.2 us (12%)
  starting transfers between devices  27.6 us (8%)
  local copies, waits for them, and re-layouts  21.4 us (6%)
  between operations  14.7 us (4%)
  other arithmetic  9.12 us (2%)
    reduce_scatter x1, waiting for transfers between devices, body(): lax.psum_scatter(weight_taps, ('ha', 'wa'), scatter_dimension=2, tiled=True)  146 us
    psum x1, waiting for transfers between devices, body(): summed = lax.psum(shared, 'ta')  73.5 us
    dot_general x27, matrix products, body(): lax.dot_general(window, flat_grad, (((0,), (0,)), ((), ())), preferred_el...  28.3 us
    ppermute x4, starting transfers between devices, with_halo(): lax.ppermute(tail, axis, [(i, (i + 1) % count) for i in range(ends)])  11.9 us
    ppermute x2, waiting for transfers between devices, from_behind(): return lax.ppermute(array, axis, pairs)  11.2 us
    ppermute x4, waiting for transfers between devices, with_halo(): lax.ppermute(tail, axis, [(i, (i + 1) % count) for i in range(ends)])  10.8 us
    another operation x1, local copies, waits for them, and re-layouts, body(): jnp.stack([lax.dot_general(window, flat_grad, (((0,), (0,)), ((), ())), p...  10.3 us
    ppermute x4, starting transfers between devices, with_halo(): lax.ppermute(head, axis, [((i + 1) % count, i) for i in range(ends)])  10.3 us
  transfers between devices with their start and end apart: 12, of which 9 were waited for; matrix products, arithmetic and copies ran while one was open for 4% of the time, Pallas kernels for 0%

commit v1 on v0

--- a/solution.py
+++ b/solution.py
@@ -88,7 +88,7 @@
         ]
     )
     shared = lax.psum_scatter(weight_taps, ("ha", "wa"), scatter_dimension=2, tiled=True)
-    summed = lax.psum(shared, "ta")
+    summed = jnp.sum(lax.all_gather(shared, "ta"), axis=0)
     voxels_all = (
         frames * height * width * lax.axis_size("ta") * lax.axis_size("ha") * lax.axis_size("wa")
     )

time: 365 us -> 340 us (0.932)
  waiting for transfers between devices: 246 us -> 201 us
  matrix products: 45.2 us -> 54.9 us
  local copies, waits for them, and re-layouts: 21.4 us -> 29.4 us
    psum x1 -> x0, waiting for transfers between devices: 73.5 us -> none  [body(): summed = lax.psum(shared, 'ta')]
    all_gather x0 -> x1, waiting for transfers between devices: none -> 27.7 us  [body(): summed = jnp.sum(lax.all_gather(shared, 'ta'), axis=0)]
    dot_general x27, matrix products: 7.99 us -> 17.5 us  [body(): jnp.dot(window, conv_weight[t_off, h_off, w_off], preferred_element_type=...]
    unnamed x13 -> x27, local copies, waits for them, and re-layouts: 3.45 us -> 7.9 us
  transfers between devices with their start and end apart: 12 -> 12, of which waited for: 9 -> 9; matrix products, arithmetic and copies ran while one was open for 4% -> 8% of each run, Pallas kernels for 0% -> 0%
where the time goes in v1:
time: 340 us; the launch traced here: 339 us
  waiting for transfers between devices  201 us (59%)
  matrix products  54.9 us (16%)
  local copies, waits for them, and re-layouts  29.4 us (9%)
  starting transfers between devices  27.6 us (8%)
  between operations  14.8 us (4%)
  other arithmetic  11.8 us (3%)
    reduce_scatter x1, waiting for transfers between devices, body(): lax.psum_scatter(weight_taps, ('ha', 'wa'), scatter_dimension=2, tiled=True)  146 us
    dot_general x27, matrix products, body(): lax.dot_general(window, flat_grad, (((0,), (0,)), ((), ())), preferred_el...  28.4 us
    all_gather x1, waiting for transfers between devices, body(): summed = jnp.sum(lax.all_gather(shared, 'ta'), axis=0)  27.7 us
    dot_general x27, matrix products, body(): jnp.dot(window, conv_weight[t_off, h_off, w_off], preferred_element_type=...  17.5 us
    ppermute x4, starting transfers between devices, with_halo(): lax.ppermute(tail, axis, [(i, (i + 1) % count) for i in range(ends)])  11.9 us
    ppermute x2, waiting for transfers between devices, from_behind(): return lax.ppermute(array, axis, pairs)  11.3 us
    ppermute x4, waiting for transfers between devices, with_halo(): lax.ppermute(tail, axis, [(i, (i + 1) % count) for i in range(ends)])  10.8 us
    ppermute x4, starting transfers between devices, with_halo(): lax.ppermute(head, axis, [((i + 1) % count, i) for i in range(ends)])  10.3 us
  transfers between devices with their start and end apart: 12, of which 9 were waited for; matrix products, arithmetic and copies ran while one was open for 8% of the time, Pallas kernels for 0%

profile of v1, /device:TPU:2, one launch (start us, length us, event | category | flops | bytes accessed | tf_op | source)
XLA Modules:
  0.0 339.0 jit_solution(9465956731847675547)
XLA Ops:
  8.2 1.3 collective-permute-start.5
  9.5 1.1 constant_dynamic-update-slice_fusion.1
  10.6 1.3 fusion.49
  11.8 6.5 %collective-permute-done.5 = bf16[2,16,16,256]{3,2,1,0:T(8,128)(2,1)S(1)} collective-permute-done((bf16[2,16,16,256]{3,2,1,0:T(8,128)(2,1)S(1)}, bf16[2,16,16,256]{3,2,1,0:T(8,128)(2,1)S(1)}, u32[]{:S(2)}, u32[]{:S(2)}) %collective-permute-start.5) | collective-permute-done | bytes 262176 | tf_op jit(solution)/shard_map/ppermute | solution.py:12
  18.3 1.3 collective-permute-start.6
  19.6 1.3 collective-permute-start.7
  21.0 4.1 %collective-permute-done.7 = bf16[6,1,16,256]{3,2,1,0:T(8,128)(2,1)S(1)} collective-permute-done((bf16[6,1,16,256]{3,2,1,0:T(8,128)(2,1)S(1)}, bf16[6,1,16,256]{3,2,1,0:T(8,128)(2,1)S(1)}, u32[]{:S(2)}, u32[]{:S(2)}) %collective-permute-start.7) | collective-permute-done | bytes 49184 | tf_op jit(solution)/shard_map/ppermute | solution.py:25
  25.3 5.8 %collective-permute-start.8 = (bf16[6,18,1,256]{3,2,1,0:T(2,128)(2,1)S(1)}, bf16[6,18,1,256]{3,2,1,0:T(2,128)(2,1)S(1)}, u32[]{:S(2)}, u32[]{:S(2)}) collective-permute-start(bf16[6,18,1,256]{3,2,1,0:T(2,128)(2,1)S(1)} %get-tuple-element.44), channel_id=1, source_target_pairs={{1,0},{2,1},{3,2},{4,3},{5,4},{6,5},{7,6},{9,8},{10,9},{11,10},{12... | collective-permute-start | bytes 165896 | tf_op jit(solution)/shard_map/ppermute | solution.py:25
  31.1 1.9 collective-permute-start.9
  34.0 5.9 %collective-permute-done.9 = bf16[6,18,1,256]{3,2,1,0:T(2,128)(2,1)S(1)} collective-permute-done((bf16[6,18,1,256]{3,2,1,0:T(2,128)(2,1)S(1)}, bf16[6,18,1,256]{3,2,1,0:T(2,128)(2,1)S(1)}, u32[]{:S(2)}, u32[]{:S(2)}) %collective-permute-start.9) | collective-permute-done | bytes 55328 | tf_op jit(solution)/shard_map/ppermute | solution.py:23
  40.7 3.3 fusion.191
  54.3 1.6 fusion.48
  55.9 3.8 %collective-permute-start = (bf16[2,16,16,256]{3,2,1,0:T(8,128)(2,1)S(1)}, bf16[2,16,16,256]{3,2,1,0:T(8,128)(2,1)S(1)}, u32[]{:S(2)}, u32[]{:S(2)}) collective-permute-start(bf16[2,16,16,256]{3,2,1,0:T(8,128)(2,1)S(1)} %slice.431), channel_id=1, source_target_pairs={{0,32},{32,64},{64,96},{96,128},{128,160},{160,192},{192,224},{1,3... | collective-permute-start | bytes 786440 | tf_op jit(solution)/shard_map/ppermute | solution.py:12
  59.7 4.8 %collective-permute-done = bf16[2,16,16,256]{3,2,1,0:T(8,128)(2,1)S(1)} collective-permute-done((bf16[2,16,16,256]{3,2,1,0:T(8,128)(2,1)S(1)}, bf16[2,16,16,256]{3,2,1,0:T(8,128)(2,1)S(1)}, u32[]{:S(2)}, u32[]{:S(2)}) %collective-permute-start) | collective-permute-done | bytes 262176 | tf_op jit(solution)/shard_map/ppermute | solution.py:12
  64.5 1.3 collective-permute-start.2
  65.8 4.5 %collective-permute-start.1 = (bf16[6,1,16,256]{3,2,1,0:T(8,128)(2,1)S(1)}, bf16[6,1,16,256]{3,2,1,0:T(8,128)(2,1)S(1)}, u32[]{:S(2)}, u32[]{:S(2)}) collective-permute-start(bf16[6,1,16,256]{3,2,1,0:T(8,128)(2,1)S(1)} %get-tuple-element.74), channel_id=1, source_target_pairs={{0,8},{8,16},{16,24},{1,9},{9,17},{17,25},{2,10},{10,18},{18,26},{... | collective-permute-start | bytes 147464 | tf_op jit(solution)/shard_map/ppermute | solution.py:23
  71.4 1.9 collective-permute-start.4
  73.3 4.1 %collective-permute-start.3 = (bf16[6,18,1,256]{3,2,1,0:T(2,128)(2,1)S(1)}, bf16[6,18,1,256]{3,2,1,0:T(2,128)(2,1)S(1)}, u32[]{:S(2)}, u32[]{:S(2)}) collective-permute-start(bf16[6,18,1,256]{3,2,1,0:T(2,128)(2,1)S(1)} %get-tuple-element.49), channel_id=1, source_target_pairs={{0,1},{1,2},{2,3},{3,4},{4,5},{5,6},{6,7},{8,9},{9,10},{10,11},{11... | collective-permute-start | bytes 165896 | tf_op jit(solution)/shard_map/ppermute | solution.py:23
  78.0 4.0 %collective-permute-done.3 = bf16[6,18,1,256]{3,2,1,0:T(2,128)(2,1)S(1)} collective-permute-done((bf16[6,18,1,256]{3,2,1,0:T(2,128)(2,1)S(1)}, bf16[6,18,1,256]{3,2,1,0:T(2,128)(2,1)S(1)}, u32[]{:S(2)}, u32[]{:S(2)}) %collective-permute-start.3) | collective-permute-done | bytes 55328 | tf_op jit(solution)/shard_map/ppermute | solution.py:23
  83.0 1.1 fusion.30
  84.1 1.1 fusion.36
  85.2 1.0 fusion.29
  86.2 1.1 fusion.28
  87.3 1.1 fusion.11
  88.3 1.1 fusion.27
  89.4 1.1 fusion.26
  90.4 1.1 fusion.35
  91.5 1.1 fusion.25
  93.6 1.0 fusion.34
  94.6 1.0 fusion.23
  95.7 1.0 fusion.22
  96.7 1.1 fusion.10
  97.8 1.1 fusion.21
  98.8 1.1 fusion.20
  99.9 1.1 fusion.33
  101.0 1.0 fusion.19
  102.0 1.0 fusion.18
  105.1 1.1 fusion.16
  106.2 1.0 fusion.15
  107.2 1.1 fusion.14
  108.3 1.1 fusion.13
  109.3 1.0 fusion.31
  110.4 1.1 fusion.12
  111.4 10.3 %copy.7 = f32[27,256,256]{1,0,2:T(8,128)} copy(f32[27,256,256]{2,1,0:T(8,128)} %fusion.12) | data formatting | bytes 14155776 | tf_op jit(solution)/shard_map/stack | solution.py:82
  123.2 1.0 copy-done.1
  125.5 1.4 fusion.194
  127.2 1.8 fusion.193
  133.6 146.0 %reduce-scatter.2.cloned.1.call-done = f32[27,256,8]{1,0,2:T(8,128)} async-done(((f32[27,256,256]{1,0,2:T(8,128)}), f32[27,256,8]{1,0,2:T(8,128)}) %reduce-scatter.2.cloned.1.call-update) | async-done | bytes 221200 | tf_op jit(solution)/shard_map/reduce_scatter | solution.py:90
  279.5 1.8 copy.8
  281.4 1.4 convolution_add_fusion.31
  282.8 1.3 convolution_add_fusion.30
  284.1 1.2 convolution_add_fusion.29
  285.3 1.2 convolution_add_fusion.28
  286.5 1.3 convolution_add_fusion.27
  287.8 1.3 convolution_add_fusion.26
  289.1 1.2 convolution_add_fusion.25
  290.3 1.3 convolution_add_fusion.24
  291.6 1.2 convolution_add_fusion.23
  292.8 1.2 convolution_add_fusion.22
  295.0 27.7 %all-gather.3.cloned.1.call-done = f32[216,256,8]{1,2,0:T(8,128)} async-done(((f32[27,256,8]{1,2,0:T(8,128)}), f32[216,256,8]{1,2,0:T(8,128)}) %all-gather.3.cloned.1.call-update) | async-done | bytes 1769488 | tf_op jit(solution)/shard_map/all_gather | solution.py:91
  322.7 2.3 reduce_sum.29
  325.0 2.0 copy.38
  327.0 2.0 broadcast_multiply_fusion
  329.0 3.2 copy.10
  (97 shorter events, 27.2 us)
Async XLA Ops:
  7.2 272.4 %reduce-scatter.2.cloned.1.call-start = ((), (), s32[]{:S(2)}) async-start(), calls=%async_computation.1 | async-start | bytes 8650752 | tf_op jit(solution)/shard_map/reduce_scatter | solution.py:90
  8.2 10.1 %collective-permute-start.5 = (bf16[2,16,16,256]{3,2,1,0:T(8,128)(2,1)S(1)}, bf16[2,16,16,256]{3,2,1,0:T(8,128)(2,1)S(1)}, u32[]{:S(2)}, u32[]{:S(2)}) collective-permute-start(bf16[2,16,16,256]{3,2,1,0:T(8,128)(2,1)S(1)} %slice.400), channel_id=1, source_target_pairs={{32,0},{64,32},{96,64},{128,96},{160,128},{192,160},{224,192},{33,... | collective-permute-start | bytes 786440 | tf_op jit(solution)/shard_map/ppermute | solution.py:12
  18.3 2.6 collective-permute-start.6
  19.6 5.5 %collective-permute-start.7 = (bf16[6,1,16,256]{3,2,1,0:T(8,128)(2,1)S(1)}, bf16[6,1,16,256]{3,2,1,0:T(8,128)(2,1)S(1)}, u32[]{:S(2)}, u32[]{:S(2)}) collective-permute-start(bf16[6,1,16,256]{3,2,1,0:T(8,128)(2,1)S(1)} %get-tuple-element.68), channel_id=1, source_target_pairs={{8,0},{16,8},{24,16},{9,1},{17,9},{25,17},{10,2},{18,10},{26,18},{... | collective-permute-start | bytes 147464 | tf_op jit(solution)/shard_map/ppermute | solution.py:25
  21.0 12.7 %copy-start = (bf16[3,3,3,256,256]{4,3,2,1,0:T(8,128)(2,1)S(1)}, bf16[3,3,3,256,256]{4,3,2,1,0:T(8,128)(2,1)}, u32[]{:S(2)}) copy-start(bf16[3,3,3,256,256]{4,3,2,1,0:T(8,128)(2,1)} %param.6) | copy-start | bytes 10616836
  25.3 8.7 %collective-permute-start.8 = (bf16[6,18,1,256]{3,2,1,0:T(2,128)(2,1)S(1)}, bf16[6,18,1,256]{3,2,1,0:T(2,128)(2,1)S(1)}, u32[]{:S(2)}, u32[]{:S(2)}) collective-permute-start(bf16[6,18,1,256]{3,2,1,0:T(2,128)(2,1)S(1)} %get-tuple-element.44), channel_id=1, source_target_pairs={{1,0},{2,1},{3,2},{4,3},{5,4},{6,5},{7,6},{9,8},{10,9},{11,10},{12... | collective-permute-start | bytes 165896 | tf_op jit(solution)/shard_map/ppermute | solution.py:25
  31.1 8.8 %collective-permute-start.9 = (bf16[6,18,1,256]{3,2,1,0:T(2,128)(2,1)S(1)}, bf16[6,18,1,256]{3,2,1,0:T(2,128)(2,1)S(1)}, u32[]{:S(2)}, u32[]{:S(2)}) collective-permute-start(bf16[6,18,1,256]{3,2,1,0:T(2,128)(2,1)S(1)} %get-tuple-element.45), channel_id=1, source_target_pairs={{0,1},{1,2},{2,3},{3,4},{4,5},{5,6},{6,7},{8,9},{9,10},{10,11},{11... | collective-permute-start | bytes 165896 | tf_op jit(solution)/shard_map/ppermute | solution.py:23
  50.8 1.0 copy-start.4
  52.5 1.0 copy-start.2
  52.5 1.0 copy-start.11
  55.9 8.6 %collective-permute-start = (bf16[2,16,16,256]{3,2,1,0:T(8,128)(2,1)S(1)}, bf16[2,16,16,256]{3,2,1,0:T(8,128)(2,1)S(1)}, u32[]{:S(2)}, u32[]{:S(2)}) collective-permute-start(bf16[2,16,16,256]{3,2,1,0:T(8,128)(2,1)S(1)} %slice.431), channel_id=1, source_target_pairs={{0,32},{32,64},{64,96},{96,128},{128,160},{160,192},{192,224},{1,3... | collective-permute-start | bytes 786440 | tf_op jit(solution)/shard_map/ppermute | solution.py:12
  64.5 5.9 %collective-permute-start.2 = (bf16[6,1,16,256]{3,2,1,0:T(8,128)(2,1)S(1)}, bf16[6,1,16,256]{3,2,1,0:T(8,128)(2,1)S(1)}, u32[]{:S(2)}, u32[]{:S(2)}) collective-permute-start(bf16[6,1,16,256]{3,2,1,0:T(8,128)(2,1)S(1)} %get-tuple-element.73), channel_id=1, source_target_pairs={{8,0},{16,8},{24,16},{9,1},{17,9},{25,17},{10,2},{18,10},{26,18},{... | collective-permute-start | bytes 147464 | tf_op jit(solution)/shard_map/ppermute | solution.py:25
  65.8 5.4 %collective-permute-start.1 = (bf16[6,1,16,256]{3,2,1,0:T(8,128)(2,1)S(1)}, bf16[6,1,16,256]{3,2,1,0:T(8,128)(2,1)S(1)}, u32[]{:S(2)}, u32[]{:S(2)}) collective-permute-start(bf16[6,1,16,256]{3,2,1,0:T(8,128)(2,1)S(1)} %get-tuple-element.74), channel_id=1, source_target_pairs={{0,8},{8,16},{16,24},{1,9},{9,17},{17,25},{2,10},{10,18},{18,26},{... | collective-permute-start | bytes 147464 | tf_op jit(solution)/shard_map/ppermute | solution.py:23
  71.4 6.6 %collective-permute-start.4 = (bf16[6,18,1,256]{3,2,1,0:T(2,128)(2,1)S(1)}, bf16[6,18,1,256]{3,2,1,0:T(2,128)(2,1)S(1)}, u32[]{:S(2)}, u32[]{:S(2)}) collective-permute-start(bf16[6,18,1,256]{3,2,1,0:T(2,128)(2,1)S(1)} %get-tuple-element.48), channel_id=1, source_target_pairs={{1,0},{2,1},{3,2},{4,3},{5,4},{6,5},{7,6},{9,8},{10,9},{11,10},{12... | collective-permute-start | bytes 165896 | tf_op jit(solution)/shard_map/ppermute | solution.py:25
  73.3 8.8 %collective-permute-start.3 = (bf16[6,18,1,256]{3,2,1,0:T(2,128)(2,1)S(1)}, bf16[6,18,1,256]{3,2,1,0:T(2,128)(2,1)S(1)}, u32[]{:S(2)}, u32[]{:S(2)}) collective-permute-start(bf16[6,18,1,256]{3,2,1,0:T(2,128)(2,1)S(1)} %get-tuple-element.49), channel_id=1, source_target_pairs={{0,1},{1,2},{2,3},{3,4},{4,5},{5,6},{6,7},{8,9},{9,10},{10,11},{11... | collective-permute-start | bytes 165896 | tf_op jit(solution)/shard_map/ppermute | solution.py:23
  121.8 200.9 %all-gather.3.cloned.1.call-start = ((), (), s32[]{:S(2)}) async-start(), calls=%async_computation.2 | async-start | bytes 1990656 | tf_op jit(solution)/shard_map/all_gather | solution.py:91
  122.0 2.2 copy-start.1
  133.3 149.6 %copy-start.7 = (bf16[4,16,16,256]{3,2,1,0:T(8,128)(2,1)S(1)}, bf16[4,16,16,256]{3,2,1,0:T(8,128)(2,1)}, u32[]{:S(2)}) copy-start(bf16[4,16,16,256]{3,2,1,0:T(8,128)(2,1)} %get-tuple-element.35) | copy-start | bytes 1572868
  281.3 2.8 copy-start.10
  281.3 4.0 %copy-start.8 = (bf16[4,16,16,256]{3,2,1,0:T(8,128)(2,1)S(1)}, bf16[4,16,16,256]{3,2,1,0:T(8,128)(2,1)}, u32[]{:S(2)}) copy-start(bf16[4,16,16,256]{3,2,1,0:T(8,128)(2,1)} %get-tuple-element.26) | copy-start | bytes 1572868
  282.8 3.7 %copy-start.6 = (bf16[4,16,16,256]{3,2,1,0:T(8,128)(2,1)S(1)}, bf16[4,16,16,256]{3,2,1,0:T(8,128)(2,1)}, u32[]{:S(2)}) copy-start(bf16[4,16,16,256]{3,2,1,0:T(8,128)(2,1)} %get-tuple-element.34) | copy-start | bytes 1572868
  286.5 3.8 %copy-start.5 = (bf16[4,16,16,256]{3,2,1,0:T(8,128)(2,1)S(1)}, bf16[4,16,16,256]{3,2,1,0:T(8,128)(2,1)}, u32[]{:S(2)}) copy-start(bf16[4,16,16,256]{3,2,1,0:T(8,128)(2,1)} %get-tuple-element.33) | copy-start | bytes 1572868
  287.8 3.8 %copy-start.9 = (bf16[4,16,16,256]{3,2,1,0:T(8,128)(2,1)S(1)}, bf16[4,16,16,256]{3,2,1,0:T(8,128)(2,1)}, u32[]{:S(2)}) copy-start(bf16[4,16,16,256]{3,2,1,0:T(8,128)(2,1)} %get-tuple-element.56) | copy-start | bytes 1572868
  290.3 3.7 %copy-start.3 = (bf16[4,16,16,256]{3,2,1,0:T(8,128)(2,1)S(1)}, bf16[4,16,16,256]{3,2,1,0:T(8,128)(2,1)}, u32[]{:S(2)}) copy-start(bf16[4,16,16,256]{3,2,1,0:T(8,128)(2,1)} %param.4) | copy-start | bytes 1572868
Sparse Core Ops, SparseCore 0:
  121.9 157.6 reduce-scatter.1
  281.9 40.7 all-gather.2
